TPU v7x, 256 devices: a whole 4x4x8 slice. The times are simulated.
256 devices in a mesh: dp: 8 (over y, core), proto: 32 (over z, x).
Axes of the slice: x: 4, y: 4, z: 8, core: 2. Of those that a mesh axis runs over, the one named last changes fastest.
Arguments:
- teacher_features: bfloat16 [6144, 384], P('dp'), may hold values from -8 to 8
- student_features: bfloat16 [6144, 384], P('dp'), may hold values from -8 to 8
- teacher_weight: bfloat16 [384, 131072], P('dp', 'proto'), may hold values from -1 to 1
- student_weight: bfloat16 [384, 131072], P('dp', 'proto'), may hold values from -1 to 1
Outputs:
- teacher_codes: bfloat16 [6144, 131072], P('dp', 'proto')
- head_loss: float32 [], replicated
- weight_grad: float32 [384, 131072], P('dp', 'proto')
All inputs are finite; a program needn't handle non-finite values.
Results may differ from a plain program's by a relative error of at most 0.003.
Values may be sent and summed in bfloat16 or wider, within the bound.
A program may use at most 128 MiB of HBM per device.

v0:
```python
import jax
import jax.numpy as jnp
from jax import lax
from jax.sharding import PartitionSpec as P

ITERS = 3
teacher_temp = 0.07
student_temp = 0.1
norm_eps = 1e-06


def column_norm(weight_rows):
    return jnp.sqrt(jnp.sum(jnp.square(weight_rows.astype(jnp.float32)), axis=0) + norm_eps)


def body(teacher_features, student_features, teacher_weight, student_weight):
    local_crops = teacher_features.shape[0]
    total_crops = local_crops * lax.axis_size("dp")
    total_protos = teacher_weight.shape[1] * lax.axis_size("proto")
    teacher_full, student_full = (
        lax.all_gather(teacher_weight, "dp", axis=0, tiled=True),
        lax.all_gather(student_weight, "dp", axis=0, tiled=True),
    )
    teacher_norm = column_norm(teacher_full)
    student_norm = column_norm(student_full)
    teacher_logits = (
        jnp.dot(teacher_features, teacher_full, preferred_element_type=jnp.float32) / teacher_norm
    )
    student_logits = (
        jnp.dot(student_features, student_full, preferred_element_type=jnp.float32) / student_norm
    )
    teacher_peak, student_peak = lax.pmax(
        (jnp.max(teacher_logits, axis=1), jnp.max(student_logits, axis=1)), "proto"
    )
    powers = jnp.exp((teacher_logits - teacher_peak[:, None]) / teacher_temp)
    shifted = (student_logits - student_peak[:, None]) / student_temp
    student_local = jnp.sum(jnp.exp(shifted), axis=1)
    crop_scale = jnp.ones((local_crops,), jnp.float32)
    for sweep_index in range(ITERS):
        proto_mass = lax.psum(jnp.dot(crop_scale, powers, precision=lax.Precision.HIGHEST), "dp")
        proto_scale = 1.0 / (total_protos * proto_mass)
        crop_local = jnp.dot(powers, proto_scale, precision=lax.Precision.HIGHEST)
        if sweep_index == 0:
            crop_mass = lax.psum(crop_local, "proto")
        else:
            crop_mass = lax.psum(crop_local, "proto")
        crop_scale = 1.0 / (total_crops * crop_mass)
    student_total = lax.psum(student_local, "proto")
    assign = powers * proto_scale[None, :] * crop_scale[:, None] * total_crops
    teacher_codes = assign.astype(jnp.bfloat16)
    log_prob = shifted - jnp.log(student_total)[:, None]
    loss_local = -jnp.sum(assign * log_prob)
    signal = ((jnp.exp(log_prob) - assign) / student_temp).astype(jnp.bfloat16)
    head_loss = lax.psum(loss_local, ("dp", "proto")) / total_crops
    own_weight = student_weight.astype(jnp.float32) / student_norm
    own_grad = lax.psum_scatter(
        lax.dot_general(
            student_features, signal, (((0,), (0,)), ((), ())), preferred_element_type=jnp.float32
        ),
        "dp",
        scatter_dimension=0,
        tiled=True,
    )
    pressure = lax.psum(jnp.sum(own_grad * own_weight, axis=0), "dp")
    weight_grad = (own_grad - own_weight * pressure[None, :]) / student_norm
    return (teacher_codes, head_loss, weight_grad)


def solution(mesh):
    return jax.shard_map(
        body,
        mesh=mesh,
        in_specs=(P("dp", None), P("dp", None), P("dp", "proto"), P("dp", "proto")),
        out_specs=(P("dp", "proto"), P(), P("dp", "proto")),
        check_vma=False,
    )
```

profile of v0, /device:TPU:32, one launch (start us, length us, event | category | flops | bytes accessed | tf_op | source)
XLA Modules:
  0.0 684.9 jit_solution(6292353373318271310)
XLA Ops:
  8.0 0.7 all-gather.3.cloned.1.call-update
  8.7 34.1 %all-gather.5.cloned.1.call-done = bf16[384,4096]{1,0:T(8,128)(2,1)} async-done(((bf16[48,4096]{1,0:T(8,128)(2,1)}), bf16[384,4096]{1,0:T(8,128)(2,1)}) %all-gather.5.cloned.1.call-update) | async-done | bytes 3145744 | tf_op jit(solution)/shard_map/all_gather | solution.py:22
  42.8 2.6 multiply_reduce_fusion.1
  45.4 29.6 %all-gather.3.cloned.1.call-done = bf16[384,4096]{1,0:T(8,128)(2,1)} async-done(((bf16[48,4096]{1,0:T(8,128)(2,1)}), bf16[384,4096]{1,0:T(8,128)(2,1)}) %all-gather.3.cloned.1.call-update) | async-done | bytes 3145744 | tf_op jit(solution)/shard_map/all_gather | solution.py:21
  75.1 2.6 multiply_reduce_fusion.2
  77.7 8.5 %fusion.9 = (f32[768]{0:T(1024)S(1)}, f32[768,4096]{1,0:T(8,128)}) fusion(f32[4096]{0:T(1024)S(1)} %add_sqrt_fusion, bf16[768,384]{1,0:T(8,128)(2,1)S(1)} %copy-done, bf16[384,4096]{1,0:T(8,128)(2,1)} %all-gather.5.cloned.1.call-done), kind=kOutput, calls=%fused_computation.33 | convolution fusion | flops 2422209792 | bytes 16337920 | tf_op jit(solution)/shard_map/dot_general | solution.py:30
  86.2 6.4 fusion.3
  92.6 70.3 %all-reduce.1 = (f32[768]{0:T(1024)S(1)}, f32[768]{0:T(1024)S(1)}) all-reduce(f32[768]{0:T(1024)S(1)} %get-tuple-element.15, f32[768]{0:T(1024)S(1)} %get-tuple-element.17), channel_id=1, replica_groups=mesh['dp'=8,'proto'=32] {'proto'}, use_global_device_ids=true, to_apply=%region_2.0 | all-reduce | flops 1536 | bytes 12288 | tf_op jit(solution)/shard_map/pmax | solution.py:32
  162.9 10.4 %exponential_reduce_fusion = (f32[768]{0:T(1024)S(1)}, f32[768,4096]{1,0:T(8,128)S(1)}) fusion(f32[768,4096]{1,0:T(8,128)} %get-tuple-element.18, f32[768]{0:T(1024)S(1)} %get-tuple-element.12, f32[768]{0:T(1024)S(1)} %get-tuple-element.11, f32[768,4096]{1,0:T(8,128)} %get-tuple-element.16, f32[4096]{0:T(1024)S(1)} %add_sqrt_fusion.1), kind=kLoop, calls=%fused_computation.2 | loop fusion | flops 18873600 | bytes 37774336 | tf_op jit(solution)/shard_map/reduce_sum | solution.py:37
  173.4 4.5 copy-done.1
  177.8 6.0 fusion.4
  183.8 24.1 %psum.63 = f32[4096]{0:T(1024)S(1)} all-reduce(f32[4096]{0:T(1024)S(1)} %bitcast.30), channel_id=1, replica_groups=mesh['dp'=8,'proto'=32] {'dp'}, use_global_device_ids=true, to_apply=%region_3.0 | all-reduce | flops 4096 | bytes 32768 | tf_op jit(solution)/shard_map/psum | solution.py:40
  207.9 13.3 %convolution_reduce_fusion.2 = f32[768]{0:T(1024)S(1)} fusion(f32[768,4096]{1,0:T(8,128)} %copy-done.1, f32[4096,1]{0,1:T(1,128)S(1)} %bitcast.26), kind=kOutput, calls=%fused_computation.19 | convolution fusion | flops 37748736 | bytes 12602368 | tf_op jit(solution)/shard_map/dot_general | solution.py:42
  221.2 69.6 %psum.64 = f32[768]{0:T(1024)S(1)} all-reduce(f32[768]{0:T(1024)S(1)} %convolution_reduce_fusion.2), channel_id=1, replica_groups=mesh['dp'=8,'proto'=32] {'proto'}, use_global_device_ids=true, to_apply=%region_4.0 | all-reduce | flops 768 | bytes 6144 | tf_op jit(solution)/shard_map/psum | solution.py:44
  290.9 8.5 %fusion.10 = f32[1,4096]{1,0:T(1,128)S(1)} fusion(f32[768,1]{0,1:T(1,128)S(1)} %reshape.24, f32[768,4096]{1,0:T(8,128)} %copy-done.1), kind=kOutput, calls=%fused_computation.34 | convolution fusion | flops 37748736 | bytes 12602368 | tf_op jit(solution)/shard_map/dot_general | solution.py:40
  299.4 23.6 %psum.65 = f32[4096]{0:T(1024)S(1)} all-reduce(f32[4096]{0:T(1024)S(1)} %bitcast.27), channel_id=1, replica_groups=mesh['dp'=8,'proto'=32] {'dp'}, use_global_device_ids=true, to_apply=%region_5.0 | all-reduce | flops 4096 | bytes 32768 | tf_op jit(solution)/shard_map/psum | solution.py:40
  323.0 13.3 %convolution_reduce_fusion.1 = f32[768]{0:T(1024)S(1)} fusion(f32[768,4096]{1,0:T(8,128)} %copy-done.1, f32[4096,1]{0,1:T(1,128)S(1)} %bitcast.28), kind=kOutput, calls=%fused_computation.18 | convolution fusion | flops 37748736 | bytes 12602368 | tf_op jit(solution)/shard_map/dot_general | solution.py:42
  336.3 71.8 %psum.66 = f32[768]{0:T(1024)S(1)} all-reduce(f32[768]{0:T(1024)S(1)} %convolution_reduce_fusion.1), channel_id=1, replica_groups=mesh['dp'=8,'proto'=32] {'proto'}, use_global_device_ids=true, to_apply=%region_6.0 | all-reduce | flops 768 | bytes 6144 | tf_op jit(solution)/shard_map/psum | solution.py:46
  408.1 8.5 %fusion.11 = f32[1,4096]{1,0:T(1,128)S(1)} fusion(f32[768,1]{0,1:T(1,128)S(1)} %reshape.28, f32[768,4096]{1,0:T(8,128)} %copy-done.1), kind=kOutput, calls=%fused_computation.35 | convolution fusion | flops 37748736 | bytes 12602368 | tf_op jit(solution)/shard_map/dot_general | solution.py:40
  416.6 23.6 %psum.67 = f32[4096]{0:T(1024)S(1)} all-reduce(f32[4096]{0:T(1024)S(1)} %bitcast.29), channel_id=1, replica_groups=mesh['dp'=8,'proto'=32] {'dp'}, use_global_device_ids=true, to_apply=%region_7.0 | all-reduce | flops 4096 | bytes 32768 | tf_op jit(solution)/shard_map/psum | solution.py:40
  440.2 13.3 %convolution_reduce_fusion = f32[768]{0:T(1024)S(1)} fusion(f32[768,4096]{1,0:T(8,128)} %copy-done.1, f32[4096,1]{0,1:T(1,128)S(1)} %bitcast.25), kind=kOutput, calls=%fused_computation.17 | convolution fusion | flops 37748736 | bytes 12602368 | tf_op jit(solution)/shard_map/dot_general | solution.py:42
  453.5 70.9 %all-reduce = (f32[768]{0:T(1024)S(1)}, f32[768]{0:T(1024)S(1)}) all-reduce(f32[768]{0:T(1024)S(1)} %convolution_reduce_fusion, f32[768]{0:T(1024)S(1)} %get-tuple-element.19), channel_id=1, replica_groups=mesh['dp'=8,'proto'=32] {'proto'}, use_global_device_ids=true, to_apply=%region_8.0 | all-reduce | flops 1536 | bytes 12288 | tf_op jit(solution)/shard_map/psum | solution.py:46
  524.4 13.1 %fusion.2 = f32[384,4096]{0,1:T(8,128)} fusion(bf16[768,384]{1,0:T(8,128)(2,1)S(1)} %copy-done, f32[768,4096]{1,0:T(8,128)} %get-tuple-element.18, f32[768,4096]{1,0:T(8,128)} %copy-done.1, f32[768]{0:T(1024)S(1)} %log.3, f32[768]{0:T(1024)S(1)} %get-tuple-element.12, f32[768]{0:T(1024)S(1)} %multiply_divide_fusion.3, f32[4096]{0:T(1024)S(1)} %multiply_divide_fusion), kind=kOutput, calls=%fused_computation.12 | convolution fusion | flops 2444230656 | bytes 32072704 | tf_op jit(solution)/shard_map/dot_general | solution.py:57
  537.5 6.5 copy.11
  544.0 14.4 %multiply_reduce_fusion = (f32[]{:T(128)}, bf16[768,4096]{1,0:T(8,128)(2,1)}) fusion(f32[768,4096]{1,0:T(8,128)} %get-tuple-element.18, f32[768,4096]{1,0:T(8,128)} %copy-done.1, f32[768]{0:T(1024)S(1)} %log.3, f32[768]{0:T(1024)S(1)} %get-tuple-element.12, f32[768]{0:T(1024)S(1)} %multiply_divide_fusion.3, f32[4096]{0:T(1024)S(1)} %multiply_divide_fusion), kind=kLoop, calls=%fused_computation.1 | loop fusion | flops 28311552 | bytes 31482884 | tf_op jit(solution)/shard_map/reduce_sum | solution.py:52
  559.1 1.3 copy.9
  560.4 80.6 %psum.70 = f32[]{:T(128)} all-reduce(f32[]{:T(128)S(6)} %neg.3), channel_id=1, replica_groups=mesh['dp'=8,'proto'=32] {'dp','proto'}, use_global_device_ids=true, to_apply=%region_15.0 | all-reduce | flops 1 | bytes 8 | tf_op jit(solution)/shard_map/psum | solution.py:54
  641.7 1.7 copy.12
  643.4 2.3 multiply_reduce_fusion.3
  645.8 23.6 %psum.71 = f32[4096]{0:T(1024)S(1)} all-reduce(f32[4096]{0:T(1024)S(1)} %multiply_reduce_fusion.3), channel_id=1, replica_groups=mesh['dp'=8,'proto'=32] {'dp'}, use_global_device_ids=true, to_apply=%region_18.0 | all-reduce | flops 4096 | bytes 32768 | tf_op jit(solution)/shard_map/psum | solution.py:64
  669.3 4.6 subtract_divide_fusion
  673.9 3.1 copy.10
  (26 shorter events, 0.9 us)
Async XLA Ops:
  7.2 70.5 %copy-start = (bf16[768,384]{1,0:T(8,128)(2,1)S(1)}, bf16[768,384]{1,0:T(8,128)(2,1)}, u32[]{:S(2)}) copy-start(bf16[768,384]{1,0:T(8,128)(2,1)} %param.5) | copy-start | bytes 1769476
  7.2 35.6 %all-gather.5.cloned.1.call-start = ((), (), s32[]{:S(2)}) async-start(), calls=%async_computation.2 | async-start | bytes 3538944 | tf_op jit(solution)/shard_map/all_gather | solution.py:22
  7.9 67.1 %all-gather.3.cloned.1.call-start = ((), (), s32[]{:S(2)}) async-start(), calls=%async_computation.1 | async-start | bytes 3538944 | tf_op jit(solution)/shard_map/all_gather | solution.py:21
  8.7 633.0 %reduce-scatter.4.cloned.1.call-start = ((), (), s32[]{:S(2)}) async-start(), calls=%async_computation.3 | async-start | bytes 7077888
  77.7 8.6 %copy-start.2 = (bf16[384,4096]{1,0:T(8,128)(2,1)S(1)}, bf16[384,4096]{1,0:T(8,128)(2,1)}, u32[]{:S(2)}) copy-start(bf16[384,4096]{1,0:T(8,128)(2,1)} %all-gather.3.cloned.1.call-done) | copy-start | bytes 9437188
  77.7 8.6 %copy-start.4 = (bf16[768,384]{1,0:T(8,128)(2,1)S(1)}, bf16[768,384]{1,0:T(8,128)(2,1)}, u32[]{:S(2)}) copy-start(bf16[768,384]{1,0:T(8,128)(2,1)} %param.4) | copy-start | bytes 1769476
  173.4 4.5 copy-start.1
  544.0 15.1 %copy-start.3 = (bf16[48,4096]{1,0:T(8,128)(2,1)S(1)}, bf16[48,4096]{1,0:T(8,128)(2,1)}, u32[]{:S(2)}) copy-start(bf16[48,4096]{1,0:T(8,128)(2,1)} %param.7) | copy-start | bytes 1179652
Sparse Core Ops, SparseCore 0:
  9.8 32.9 all-gather.4
  44.6 30.3 all-gather.2
  544.2 46.9 reduce-scatter.3
where the time goes:
time: 689 us; the launch traced here: 685 us
  blocking collectives  458 us (66%)
  matrix products  91 us (13%)
  waiting for transfers between devices  65.2 us (9%)
  other arithmetic  37 us (5%)
  local copies, waits for them, and re-layouts  17.1 us (2%)
  between operations  16.6 us (2%)
    psum x3, blocking collectives, body(): crop_mass = lax.psum(crop_local, 'proto')  212 us
    psum x1, blocking collectives, body(): head_loss = lax.psum(loss_local, ('dp', 'proto')) / total_crops  80.6 us
    psum x3, blocking collectives, body(): lax.psum(jnp.dot(crop_scale, powers, precision=lax.Precision.HIGHEST), 'dp')  71.2 us
    pmax x1, blocking collectives, body(): lax.pmax((jnp.max(teacher_logits, axis=1), jnp.max(student_logits, axis=1...  70.3 us
    dot_general x3, matrix products, body(): crop_local = jnp.dot(powers, proto_scale, precision=lax.Precision.HIGHEST)  39.9 us
    all_gather x1, waiting for transfers between devices, body(): lax.all_gather(student_weight, 'dp', axis=0, tiled=True)  34.1 us
    all_gather x1, waiting for transfers between devices, body(): lax.all_gather(teacher_weight, 'dp', axis=0, tiled=True)  29.6 us
    psum x1, blocking collectives, body(): pressure = lax.psum(jnp.sum(own_grad * own_weight, axis=0), 'dp')  23.6 us
  transfers between devices with their start and end apart: 3, of which 2 were waited for; matrix products, arithmetic and copies ran while one was open for 3% of the time, Pallas kernels for 0%

commit v1 on v0

--- a/solution.py
+++ b/solution.py
@@ -41,7 +41,11 @@
         proto_scale = 1.0 / (total_protos * proto_mass)
         crop_local = jnp.dot(powers, proto_scale, precision=lax.Precision.HIGHEST)
         if sweep_index == 0:
-            crop_mass = lax.psum(crop_local, "proto")
+
+            def _touch_vectors(field_in, axis_tag):
+                return lax.all_gather(field_in, axis_name=axis_tag).sum(axis=0)
+
+            crop_mass = _touch_vectors(crop_local, "proto")
         else:
             crop_mass = lax.psum(crop_local, "proto")
         crop_scale = 1.0 / (total_crops * crop_mass)

time: 689 us -> 660 us (0.958)
  blocking collectives: 458 us -> 429 us
    psum x3 -> x2, blocking collectives: 212 us -> 137 us  [body(): crop_mass = lax.psum(crop_local, 'proto')]
    all_gather x0 -> x1, blocking collectives: none -> 46.5 us  [_touch_vectors(): return lax.all_gather(field_in, axis_name=axis_tag).sum(axis=0)]
where the time goes in v1:
time: 660 us; the launch traced here: 656 us
  blocking collectives  429 us (65%)
  matrix products  91 us (14%)
  waiting for transfers between devices  65.2 us (10%)
  other arithmetic  37 us (6%)
  local copies, waits for them, and re-layouts  17.1 us (3%)
  between operations  16.6 us (3%)
    psum x2, blocking collectives, body(): crop_mass = lax.psum(crop_local, 'proto')  137 us
    psum x1, blocking collectives, body(): head_loss = lax.psum(loss_local, ('dp', 'proto')) / total_crops  80.6 us
    psum x3, blocking collectives, body(): lax.psum(jnp.dot(crop_scale, powers, precision=lax.Precision.HIGHEST), 'dp')  71.2 us
    pmax x1, blocking collectives, body(): lax.pmax((jnp.max(teacher_logits, axis=1), jnp.max(student_logits, axis=1...  70.3 us
    all_gather x1, blocking collectives, _touch_vectors(): return lax.all_gather(field_in, axis_name=axis_tag).sum(axis=0)  46.5 us
    dot_general x3, matrix products, body(): crop_local = jnp.dot(powers, proto_scale, precision=lax.Precision.HIGHEST)  39.9 us
    all_gather x1, waiting for transfers between devices, body(): lax.all_gather(student_weight, 'dp', axis=0, tiled=True)  34.1 us
    all_gather x1, waiting for transfers between devices, body(): lax.all_gather(teacher_weight, 'dp', axis=0, tiled=True)  29.6 us
  transfers between devices with their start and end apart: 3, of which 2 were waited for; matrix products, arithmetic and copies ran while one was open for 3% of the time, Pallas kernels for 0%

profile of v1, /device:TPU:32, one launch (start us, length us, event | category | flops | bytes accessed | tf_op | source)
XLA Modules:
  0.0 655.7 jit_solution(17613432501952067862)
XLA Ops:
  8.0 0.7 all-gather.5.cloned.1.call-update
  8.7 34.1 %all-gather.7.cloned.1.call-done = bf16[384,4096]{1,0:T(8,128)(2,1)} async-done(((bf16[48,4096]{1,0:T(8,128)(2,1)}), bf16[384,4096]{1,0:T(8,128)(2,1)}) %all-gather.7.cloned.1.call-update) | async-done | bytes 3145744 | tf_op jit(solution)/shard_map/all_gather | solution.py:22
  42.8 2.6 multiply_reduce_fusion.1
  45.4 29.6 %all-gather.5.cloned.1.call-done = bf16[384,4096]{1,0:T(8,128)(2,1)} async-done(((bf16[48,4096]{1,0:T(8,128)(2,1)}), bf16[384,4096]{1,0:T(8,128)(2,1)}) %all-gather.5.cloned.1.call-update) | async-done | bytes 3145744 | tf_op jit(solution)/shard_map/all_gather | solution.py:21
  75.1 2.6 multiply_reduce_fusion.2
  77.7 8.5 %fusion.9 = (f32[768]{0:T(1024)S(1)}, f32[768,4096]{1,0:T(8,128)}) fusion(f32[4096]{0:T(1024)S(1)} %add_sqrt_fusion, bf16[768,384]{1,0:T(8,128)(2,1)S(1)} %copy-done, bf16[384,4096]{1,0:T(8,128)(2,1)} %all-gather.7.cloned.1.call-done), kind=kOutput, calls=%fused_computation.33 | convolution fusion | flops 2422209792 | bytes 16337920 | tf_op jit(solution)/shard_map/dot_general | solution.py:30
  86.2 6.4 fusion.3
  92.6 70.3 %all-reduce.1 = (f32[768]{0:T(1024)S(1)}, f32[768]{0:T(1024)S(1)}) all-reduce(f32[768]{0:T(1024)S(1)} %get-tuple-element.15, f32[768]{0:T(1024)S(1)} %get-tuple-element.17), channel_id=1, replica_groups=mesh['dp'=8,'proto'=32] {'proto'}, use_global_device_ids=true, to_apply=%region_2.0 | all-reduce | flops 1536 | bytes 12288 | tf_op jit(solution)/shard_map/pmax | solution.py:32
  162.9 10.4 %exponential_reduce_fusion = (f32[768]{0:T(1024)S(1)}, f32[768,4096]{1,0:T(8,128)S(1)}) fusion(f32[768,4096]{1,0:T(8,128)} %get-tuple-element.18, f32[768]{0:T(1024)S(1)} %get-tuple-element.12, f32[768]{0:T(1024)S(1)} %get-tuple-element.11, f32[768,4096]{1,0:T(8,128)} %get-tuple-element.16, f32[4096]{0:T(1024)S(1)} %add_sqrt_fusion.1), kind=kLoop, calls=%fused_computation.2 | loop fusion | flops 18873600 | bytes 37774336 | tf_op jit(solution)/shard_map/reduce_sum | solution.py:37
  173.4 4.5 copy-done.1
  177.8 6.0 fusion.4
  183.8 24.1 %psum.56 = f32[4096]{0:T(1024)S(1)} all-reduce(f32[4096]{0:T(1024)S(1)} %bitcast.32), channel_id=1, replica_groups=mesh['dp'=8,'proto'=32] {'dp'}, use_global_device_ids=true, to_apply=%region_3.0 | all-reduce | flops 4096 | bytes 32768 | tf_op jit(solution)/shard_map/psum | solution.py:40
  207.9 13.3 %convolution_bitcast_fusion = f32[1,1,768]{2,1,0:T(1,128)S(1)} fusion(f32[768,4096]{1,0:T(8,128)} %copy-done.1, f32[4096,1]{0,1:T(1,128)S(1)} %bitcast.28), kind=kOutput, calls=%fused_computation.19 | convolution fusion | flops 37748736 | bytes 12602368 | tf_op jit(solution)/shard_map/dot_general | solution.py:42
  221.2 46.5 %all-gather.1 = f32[32,1,768]{2,1,0:T(1,128)S(1)} all-gather(f32[1,1,768]{2,1,0:T(1,128)S(1)} %convolution_bitcast_fusion), channel_id=2, replica_groups=mesh['dp'=8,'proto'=32] {'proto'}, dimensions={0}, use_global_device_ids=true | all-gather | bytes 101376 | tf_op jit(solution)/shard_map/all_gather | solution.py:46
  267.7 8.5 %fusion.10 = f32[1,4096]{1,0:T(1,128)S(1)} fusion(f32[768,1]{0,1:T(1,128)S(1)} %reshape.28, f32[768,4096]{1,0:T(8,128)} %copy-done.1), kind=kOutput, calls=%fused_computation.34 | convolution fusion | flops 37748736 | bytes 12602368 | tf_op jit(solution)/shard_map/dot_general | solution.py:40
  276.3 23.6 %psum.57 = f32[4096]{0:T(1024)S(1)} all-reduce(f32[4096]{0:T(1024)S(1)} %bitcast.29), channel_id=1, replica_groups=mesh['dp'=8,'proto'=32] {'dp'}, use_global_device_ids=true, to_apply=%region_5.0 | all-reduce | flops 4096 | bytes 32768 | tf_op jit(solution)/shard_map/psum | solution.py:40
  299.8 13.3 %convolution_reduce_fusion.1 = f32[768]{0:T(1024)S(1)} fusion(f32[768,4096]{1,0:T(8,128)} %copy-done.1, f32[4096,1]{0,1:T(1,128)S(1)} %bitcast.30), kind=kOutput, calls=%fused_computation.18 | convolution fusion | flops 37748736 | bytes 12602368 | tf_op jit(solution)/shard_map/dot_general | solution.py:42
  313.1 65.8 %psum.58 = f32[768]{0:T(1024)S(1)} all-reduce(f32[768]{0:T(1024)S(1)} %convolution_reduce_fusion.1), channel_id=1, replica_groups=mesh['dp'=8,'proto'=32] {'proto'}, use_global_device_ids=true, to_apply=%region_6.0 | all-reduce | flops 768 | bytes 6144 | tf_op jit(solution)/shard_map/psum | solution.py:50
  378.9 8.5 %fusion.11 = f32[1,4096]{1,0:T(1,128)S(1)} fusion(f32[768,1]{0,1:T(1,128)S(1)} %reshape.32, f32[768,4096]{1,0:T(8,128)} %copy-done.1), kind=kOutput, calls=%fused_computation.35 | convolution fusion | flops 37748736 | bytes 12602368 | tf_op jit(solution)/shard_map/dot_general | solution.py:40
  387.5 23.6 %psum.59 = f32[4096]{0:T(1024)S(1)} all-reduce(f32[4096]{0:T(1024)S(1)} %bitcast.31), channel_id=1, replica_groups=mesh['dp'=8,'proto'=32] {'dp'}, use_global_device_ids=true, to_apply=%region_7.0 | all-reduce | flops 4096 | bytes 32768 | tf_op jit(solution)/shard_map/psum | solution.py:40
  411.0 13.3 %convolution_reduce_fusion = f32[768]{0:T(1024)S(1)} fusion(f32[768,4096]{1,0:T(8,128)} %copy-done.1, f32[4096,1]{0,1:T(1,128)S(1)} %bitcast.27), kind=kOutput, calls=%fused_computation.17 | convolution fusion | flops 37748736 | bytes 12602368 | tf_op jit(solution)/shard_map/dot_general | solution.py:42
  424.3 70.9 %all-reduce = (f32[768]{0:T(1024)S(1)}, f32[768]{0:T(1024)S(1)}) all-reduce(f32[768]{0:T(1024)S(1)} %convolution_reduce_fusion, f32[768]{0:T(1024)S(1)} %get-tuple-element.19), channel_id=1, replica_groups=mesh['dp'=8,'proto'=32] {'proto'}, use_global_device_ids=true, to_apply=%region_8.0 | all-reduce | flops 1536 | bytes 12288 | tf_op jit(solution)/shard_map/psum | solution.py:50
  495.2 13.1 %fusion.2 = f32[384,4096]{0,1:T(8,128)} fusion(bf16[768,384]{1,0:T(8,128)(2,1)S(1)} %copy-done, f32[768,4096]{1,0:T(8,128)} %get-tuple-element.18, f32[768,4096]{1,0:T(8,128)} %copy-done.1, f32[768]{0:T(1024)S(1)} %log.3, f32[768]{0:T(1024)S(1)} %get-tuple-element.12, f32[768]{0:T(1024)S(1)} %multiply_divide_fusion.3, f32[4096]{0:T(1024)S(1)} %multiply_divide_fusion), kind=kOutput, calls=%fused_computation.12 | convolution fusion | flops 2444230656 | bytes 32072704 | tf_op jit(solution)/shard_map/dot_general | solution.py:61
  508.3 6.5 copy.11
  514.9 14.4 %multiply_reduce_fusion = (f32[]{:T(128)}, bf16[768,4096]{1,0:T(8,128)(2,1)}) fusion(f32[768,4096]{1,0:T(8,128)} %get-tuple-element.18, f32[768,4096]{1,0:T(8,128)} %copy-done.1, f32[768]{0:T(1024)S(1)} %log.3, f32[768]{0:T(1024)S(1)} %get-tuple-element.12, f32[768]{0:T(1024)S(1)} %multiply_divide_fusion.3, f32[4096]{0:T(1024)S(1)} %multiply_divide_fusion), kind=kLoop, calls=%fused_computation.1 | loop fusion | flops 28311552 | bytes 31482884 | tf_op jit(solution)/shard_map/reduce_sum | solution.py:56
  529.9 1.3 copy.9
  531.3 80.6 %psum.62 = f32[]{:T(128)} all-reduce(f32[]{:T(128)S(6)} %neg.3), channel_id=1, replica_groups=mesh['dp'=8,'proto'=32] {'dp','proto'}, use_global_device_ids=true, to_apply=%region_15.0 | all-reduce | flops 1 | bytes 8 | tf_op jit(solution)/shard_map/psum | solution.py:58
  612.5 1.7 copy.12
  614.2 2.3 multiply_reduce_fusion.3
  616.6 23.6 %psum.63 = f32[4096]{0:T(1024)S(1)} all-reduce(f32[4096]{0:T(1024)S(1)} %multiply_reduce_fusion.3), channel_id=1, replica_groups=mesh['dp'=8,'proto'=32] {'dp'}, use_global_device_ids=true, to_apply=%region_18.0 | all-reduce | flops 4096 | bytes 32768 | tf_op jit(solution)/shard_map/psum | solution.py:68
  640.2 4.6 subtract_divide_fusion
  644.8 3.1 copy.10
  (27 shorter events, 1.0 us)
Async XLA Ops:
  7.2 70.5 %copy-start = (bf16[768,384]{1,0:T(8,128)(2,1)S(1)}, bf16[768,384]{1,0:T(8,128)(2,1)}, u32[]{:S(2)}) copy-start(bf16[768,384]{1,0:T(8,128)(2,1)} %param.5) | copy-start | bytes 1769476
  7.2 35.6 %all-gather.7.cloned.1.call-start = ((), (), s32[]{:S(2)}) async-start(), calls=%async_computation.2 | async-start | bytes 3538944 | tf_op jit(solution)/shard_map/all_gather | solution.py:22
  7.9 67.1 %all-gather.5.cloned.1.call-start = ((), (), s32[]{:S(2)}) async-start(), calls=%async_computation.1 | async-start | bytes 3538944 | tf_op jit(solution)/shard_map/all_gather | solution.py:21
  8.7 603.8 %reduce-scatter.4.cloned.1.call-start = ((), (), s32[]{:S(2)}) async-start(), calls=%async_computation.3 | async-start | bytes 7077888
  77.7 8.6 %copy-start.2 = (bf16[384,4096]{1,0:T(8,128)(2,1)S(1)}, bf16[384,4096]{1,0:T(8,128)(2,1)}, u32[]{:S(2)}) copy-start(bf16[384,4096]{1,0:T(8,128)(2,1)} %all-gather.5.cloned.1.call-done) | copy-start | bytes 9437188
  77.7 8.6 %copy-start.4 = (bf16[768,384]{1,0:T(8,128)(2,1)S(1)}, bf16[768,384]{1,0:T(8,128)(2,1)}, u32[]{:S(2)}) copy-start(bf16[768,384]{1,0:T(8,128)(2,1)} %param.4) | copy-start | bytes 1769476
  173.4 4.5 copy-start.1
  514.9 15.1 %copy-start.3 = (bf16[48,4096]{1,0:T(8,128)(2,1)S(1)}, bf16[48,4096]{1,0:T(8,128)(2,1)}, u32[]{:S(2)}) copy-start(bf16[48,4096]{1,0:T(8,128)(2,1)} %param.7) | copy-start | bytes 1179652
Sparse Core Ops, SparseCore 0:
  9.8 32.9 all-gather.6
  44.6 30.3 all-gather.4
  515.0 46.9 reduce-scatter.3
